TPU v7x, 512 devices: a whole 4x4x16 slice. The times are simulated.
512 devices in a mesh: gx: 32 (over z, y_lo), gy: 16 (over y_hi, x, core).
Axes of the slice: x: 4, y: 4 (y_hi: 2, y_lo: 2; y = y_hi * 2 + y_lo), z: 16, core: 2. Of those that a mesh axis runs over, the one named last changes fastest.
Arguments:
- fields: float32 [5, 4, 1024, 2048], P(None, None, 'gx', 'gy'), may hold values from -6 to 6
- viscosity: float32 [4, 1024, 2048], P(None, 'gx', 'gy'), may hold values from 0.03 to 0.3
- precursor: float32 [5, 4, 512], P(None, None, 'gy'), may hold values from -6 to 6
- tile_index: int32 [2048], P('gy'), may hold values from 0 to 511, as said below
- fine_fields: float32 [8192, 5, 4, 4, 256], P(('gx', 'gy')), may hold values from -6 to 6
- fine_viscosity: float32 [8192, 4, 4, 256], P(('gx', 'gy')), may hold values from 0.03 to 0.3
- partner_gx: int32 [8192], P(('gx', 'gy')), may hold values from 0 to 31, as said below
- partner_col: int32 [8192], P(('gx', 'gy')), may hold values from 0 to 31
Outputs:
- fields_out: float32 [5, 4, 1024, 2048], P(None, None, 'gx', 'gy')
- fine_out: float32 [8192, 5, 4, 4, 256], P(('gx', 'gy'))
Inputs may be any that keep to these rules, and one draw needn't show every extreme that they name: `tile_index`: inlet cell y takes precursor cell (y + s) mod 512, where s is drawn for each aligned block of 128 cells. `partner_gx`: each device's tiles are glued to outer devices of its own gy row: exactly 2 tiles to each of 8 distinct gx indices; in every gy row one gx index receives 2 tiles from every device of the row.
All inputs are finite; a program needn't handle non-finite values.
Results may differ from a plain program's by a relative error of at most 0.00005.
Values sent between devices are 32-bit elements; how exact they have to be, the bound alone decides.
No kernel may reach another device: no remote copies, remote signals or barrier semaphores. Data moves between devices by JAX's collectives and lax.ppermute only.
A program may use at most 64 MiB of HBM per device.

v0:
```python
import jax
import jax.numpy as jnp
from jax import lax
from jax.sharding import PartitionSpec as P

CAP = 2
time_step = 0.2
vertical_mix = 0.1
coarse_penalty = 0.5
fine_penalty = 1.0


def padded_2(cells, sides, width):
    for axis, dim in sides:
        count = lax.axis_size(axis)
        head = lax.slice_in_dim(cells, 0, width, axis=dim)
        tail = lax.slice_in_dim(cells, cells.shape[dim] - width, cells.shape[dim], axis=dim)
        cells = jnp.concatenate(
            [
                lax.ppermute(tail, axis, [(i, (i + 1) % count) for i in range(count)]),
                cells,
                lax.ppermute(head, axis, [((i + 1) % count, i) for i in range(count)]),
            ],
            axis=dim,
        )
    return cells


def tendency(padded, spacing):
    nfield = padded.shape[-4] - 1
    state_part = padded[..., :nfield, :, :, :]
    visc_part = padded[..., nfield:, :, :, :]
    centre = state_part[..., 1:-1, 1:-1]
    q_east = state_part[..., 2:, 1:-1]
    q_west = state_part[..., :-2, 1:-1]
    q_north = state_part[..., 1:-1, 2:]
    q_south = state_part[..., 1:-1, :-2]
    u_flow = centre[..., 0:1, :, :, :]
    v_flow = centre[..., 1:2, :, :, :]
    nu_mid = visc_part[..., 1:-1, 1:-1]
    nu_east = 0.5 * (nu_mid + visc_part[..., 2:, 1:-1])
    nu_west = 0.5 * (nu_mid + visc_part[..., :-2, 1:-1])
    nu_north = 0.5 * (nu_mid + visc_part[..., 1:-1, 2:])
    nu_south = 0.5 * (nu_mid + visc_part[..., 1:-1, :-2])
    advect = (u_flow * (q_east - q_west) + v_flow * (q_north - q_south)) / (2.0 * spacing)
    diffuse = (
        nu_east * (q_east - centre)
        - nu_west * (centre - q_west)
        + nu_north * (q_north - centre)
        - nu_south * (centre - q_south)
    ) / (spacing * spacing)
    q_above = jnp.concatenate([centre[..., 1:, :, :], centre[..., -1:, :, :]], axis=-3)
    q_below = jnp.concatenate([centre[..., :1, :, :], centre[..., :-1, :, :]], axis=-3)
    return diffuse - advect + vertical_mix * (q_above - 2.0 * centre + q_below)


def coarsen_table(fine_width):
    fine_pos = jnp.arange(fine_width, dtype=jnp.int32)[:, None]
    coarse_pos = jnp.arange(fine_width // 2, dtype=jnp.int32)[None, :]
    weights = (
        0.5 * (fine_pos == 2 * coarse_pos)
        + 0.25 * (fine_pos == 2 * coarse_pos + 1)
        + 0.25 * (fine_pos == 2 * coarse_pos - 1)
        + 0.25 * ((coarse_pos == 0) & (fine_pos == 0))
    )
    return weights.astype(jnp.float32)


def refine_table(coarse_width):
    coarse_pos = jnp.arange(coarse_width, dtype=jnp.int32)[:, None]
    fine_pos = jnp.arange(2 * coarse_width, dtype=jnp.int32)[None, :]
    half_pos = fine_pos // 2
    upper_pos = jnp.minimum(half_pos + 1, coarse_width - 1)
    is_even = fine_pos % 2 == 0
    weights = jnp.where(
        is_even,
        1.0 * (coarse_pos == half_pos),
        0.5 * (coarse_pos == half_pos) + 0.5 * (coarse_pos == upper_pos),
    )
    return weights.astype(jnp.float32)


def on_device(
    fields, viscosity, precursor, tile_index, fine_fields, fine_viscosity, partner_gx, partner_col
):
    highest = lax.Precision.HIGHEST
    nfield, levels, columns, span_cells = fields.shape
    plane_total = precursor.shape[2] * lax.axis_size("gy")
    choose = (tile_index[:, None] == jnp.arange(plane_total, dtype=jnp.int32)[None, :]).astype(
        jnp.float32
    )
    inflow = jnp.einsum(
        "fzp,yp->fzy",
        lax.all_gather(precursor, "gy", axis=2, tiled=True),
        choose,
        precision=highest,
    )
    stacked = jnp.concatenate([fields, viscosity[None]], axis=0)
    padded = padded_2(stacked, (("gx", 2), ("gy", 3)), 1)
    at_inlet = lax.axis_index("gx") == 0
    at_outlet = lax.axis_index("gx") == lax.axis_size("gx") - 1
    inlet_ghost = jnp.concatenate([inflow, viscosity[None, :, 0, :]], axis=0)
    padded = padded.at[:, :, 0, 1:-1].set(jnp.where(at_inlet, inlet_ghost, padded[:, :, 0, 1:-1]))
    padded = padded.at[:, :, -1, 1:-1].set(
        jnp.where(at_outlet, stacked[:, :, -1, :], padded[:, :, -1, 1:-1])
    )
    coarse_rate = tendency(padded, 1.0)
    fine_stack = jnp.concatenate([fine_fields, fine_viscosity[:, None]], axis=1)
    fine_rate = tendency(
        jnp.pad(fine_stack, ((0, 0), (0, 0), (0, 0), (1, 1), (1, 1)), mode="edge"), 0.5
    )
    groups = lax.axis_size("gx")
    slot_count = groups * CAP
    target_hot = (partner_gx[:, None] == jnp.arange(groups, dtype=jnp.int32)[None, :]).astype(
        jnp.int32
    )
    before = jnp.cumsum(target_hot, axis=0) - target_hot
    rank_within = jnp.sum(before * target_hot, axis=1)
    slot_index = partner_gx * CAP + rank_within
    packing = (slot_index[:, None] == jnp.arange(slot_count, dtype=jnp.int32)[None, :]).astype(
        jnp.float32
    )
    col_hot = (partner_col[:, None] == jnp.arange(columns, dtype=jnp.int32)[None, :]).astype(
        jnp.float32
    )
    fine_trace = fine_fields[:, :, :, 0, :]
    to_coarse = coarsen_table(fine_trace.shape[-1])
    to_fine = refine_table(span_cells)
    sending = jnp.einsum("ts,tfzk->sfzk", packing, fine_trace, precision=highest)
    sending = sending.reshape((groups, CAP) + fine_trace.shape[1:])
    columns_out = jnp.einsum("ts,tc->sc", packing, col_hot, precision=highest).reshape(
        groups, CAP, columns
    )
    trace_in = lax.all_to_all(sending, "gx", split_axis=0, concat_axis=0, tiled=True)
    column_in = lax.all_to_all(columns_out, "gx", split_axis=0, concat_axis=0, tiled=True)
    coarse_in = jnp.einsum("gsfzw,wk->gsfzk", trace_in, to_coarse, precision=highest)
    matched = jnp.einsum("gsx,fzxy->gsfzy", column_in, fields, precision=highest)
    answer = jnp.einsum("gsfzk,kw->gsfzw", matched, to_fine, precision=highest)
    returned = lax.all_to_all(answer, "gx", split_axis=0, concat_axis=0, tiled=True)
    mismatch, column_in, returned = (coarse_in - matched, column_in, returned)
    coarse_sat = coarse_penalty * jnp.einsum(
        "gsx,gsfzy->fzxy", column_in, mismatch, precision=highest
    )
    fields_out = fields + time_step * (coarse_rate + coarse_sat)
    coming_back = jnp.einsum(
        "ts,sfzw->tfzw",
        packing,
        returned.reshape((slot_count,) + returned.shape[2:]),
        precision=highest,
    )
    fine_sat = fine_penalty * (coming_back - fine_trace)
    total_rate = fine_rate.at[:, :, :, 0, :].add(fine_sat)
    fine_out = fine_fields + time_step * total_rate
    return (fields_out, fine_out)


def solution(mesh):
    return jax.shard_map(
        on_device,
        mesh=mesh,
        in_specs=(
            P(None, None, "gx", "gy"),
            P(None, "gx", "gy"),
            P(None, None, "gy"),
            P("gy"),
            P(("gx", "gy"), None, None, None, None),
            P(("gx", "gy"), None, None, None),
            P(("gx", "gy")),
            P(("gx", "gy")),
        ),
        out_specs=(P(None, None, "gx", "gy"), P(("gx", "gy"), None, None, None, None)),
        check_vma=False,
    )
```

profile of v0, /device:TPU:58, one launch (start us, length us, event | category | flops | bytes accessed | tf_op | source)
XLA Modules:
  0.0 180.7 jit_solution(5967769567230981480)
XLA Ops:
  0.6 0.7 fusion.91
  1.4 0.8 select_reduce_fusion
  2.9 1.6 fusion.89
  4.5 16.3 %all-to-all-start.1 = ((f32[32,2,32]{2,1,0:T(2,128)}), f32[32,2,32]{2,1,0:T(2,128)S(1)}, u32[]{:S(2)}, u32[]{:S(2)}) async-start(f32[32,2,32]{2,1,0:T(2,128)} %bitcast.19), calls=%async_computation.1 | async-start | bytes 65536 | tf_op jit(solution)/shard_map/all_to_all | solution.py:135
  20.7 2.1 %copy.142 = f32[16,5,4,4,256]{4,0,2,1,3:T(8,128)S(1)} copy(f32[16,5,4,4,256]{4,3,2,1,0:T(4,128)} %param.18) | data formatting | bytes 2621440 | tf_op args[4]
  22.8 0.8 fusion.31
  23.6 1.9 %copy.143 = f32[32,2,5,4,256]{4,3,2,1,0:T(4,128)} copy(f32[32,2,5,4,256]{4,0,3,2,1:T(8,128)S(1)} %fusion.31) | data formatting | bytes 2621440 | tf_op jit(solution)/shard_map/ts,tfzk->sfzk/dot_general | solution.py:129
  25.5 6.8 %all-to-all-done.1 = f32[32,2,32]{2,1,0:T(2,128)S(1)} async-done(((f32[32,2,32]{2,1,0:T(2,128)}), f32[32,2,32]{2,1,0:T(2,128)S(1)}, u32[]{:S(2)}, u32[]{:S(2)}) %all-to-all-start.1) | async-done | bytes 8224 | tf_op jit(solution)/shard_map/all_to_all | solution.py:135
  32.3 6.5 %all-to-all-start = ((f32[32,2,5,4,256]{4,3,2,1,0:T(4,128)}), f32[32,2,5,4,256]{4,3,2,1,0:T(4,128)}, u32[]{:S(2)}, u32[]{:S(2)}) async-start(f32[32,2,5,4,256]{4,3,2,1,0:T(4,128)} %copy.143), calls=%async_computation | async-start | bytes 2621440 | tf_op jit(solution)/shard_map/all_to_all | solution.py:134
  38.8 3.4 %collective-permute-start = (f32[6,4,1,128]{3,2,1,0:T(1,128)S(1)}, f32[6,4,1,128]{3,2,1,0:T(1,128)S(1)}, u32[]{:S(2)}, u32[]{:S(2)}) collective-permute-start(f32[6,4,1,128]{3,2,1,0:T(1,128)S(1)} %get-tuple-element.74), channel_id=1, source_target_pairs={{0,16},{16,32},{32,48},{48,64},{64,80},{80,96},{96,112},{112,128},... | collective-permute-start | bytes 36872 | tf_op jit(solution)/shard_map/ppermute | solution.py:20
  42.2 2.5 %collective-permute-start.1 = (f32[6,4,1,128]{3,2,1,0:T(1,128)S(1)}, f32[6,4,1,128]{3,2,1,0:T(1,128)S(1)}, u32[]{:S(2)}, u32[]{:S(2)}) collective-permute-start(f32[6,4,1,128]{3,2,1,0:T(1,128)S(1)} %get-tuple-element.75), channel_id=1, source_target_pairs={{16,0},{32,16},{48,32},{64,48},{80,64},{96,80},{112,96},{128,112},... | collective-permute-start | bytes 36872 | tf_op jit(solution)/shard_map/ppermute | solution.py:22
  44.9 1.1 slice_bitcast_fusion.1
  46.4 24.0 %all_gather.3 = f32[5,4,512]{0,1,2:T(4,128)} all-gather(f32[5,4,32]{0,1,2:T(4,128)S(1)} %copy.138), channel_id=1, replica_groups=mesh['gx'=32,'gy'=16] {'gy'}, dimensions={2}, use_global_device_ids=true | all-gather | bytes 43520 | tf_op jit(solution)/shard_map/all_gather | solution.py:94
  70.4 1.6 copy.167
  73.4 1.2 fusion.49
  74.6 1.9 %copy.163 = f32[32,2,5,4,256]{4,3,2,1,0:T(4,128)} copy(f32[32,2,5,4,256]{4,0,3,2,1:T(8,128)S(1)} %fusion.49) | data formatting | bytes 2621440 | tf_op jit(solution)/shard_map/gsfzk,kw->gsfzw/dot_general | solution.py:138
  76.5 27.4 %all-to-all-done = f32[32,2,5,4,256]{4,3,2,1,0:T(4,128)} async-done(((f32[32,2,5,4,256]{4,3,2,1,0:T(4,128)}), f32[32,2,5,4,256]{4,3,2,1,0:T(4,128)}, u32[]{:S(2)}, u32[]{:S(2)}) %all-to-all-start) | async-done | bytes 1310752 | tf_op jit(solution)/shard_map/all_to_all | solution.py:134
  103.9 4.6 %all-to-all-start.2 = ((f32[32,2,5,4,256]{4,3,2,1,0:T(4,128)}), f32[32,2,5,4,256]{4,3,2,1,0:T(4,128)}, u32[]{:S(2)}, u32[]{:S(2)}) async-start(f32[32,2,5,4,256]{4,3,2,1,0:T(4,128)} %copy.163), calls=%async_computation.2 | async-start | bytes 2621440 | tf_op jit(solution)/shard_map/all_to_all | solution.py:139
  110.6 3.0 %fusion.2 = f32[16,5,4,4,256]{4,0,2,1,3:T(8,128)} fusion(f32[16,5,1,4,256]{4,0,2,1,3:T(8,128)S(1)} %get-tuple-element.59, f32[16,5,3,4,256]{4,0,2,1,3:T(8,128)S(1)} %get-tuple-element.61, f32[16,5,3,4,256]{4,0,2,1,3:T(8,128)S(1)} %get-tuple-element.60, f32[16,5,1,4,256]{4,0,2,1,3:T(8,128)S(1)} %get-tuple-element.58, f32[16,5,4,4,256]{4,0,2,1,3:T(8,128)S(1)} %copy.142, ...), kind=kLoop, calls=%fused_computation.16 | loop fusion | flops 12124160 | bytes 7882752 | tf_op jit(solution)/shard_map/add | solution.py:54
  114.1 1.9 %collective-permute-start.2 = (f32[6,4,34,1]{2,1,3,0:T(4,128)S(1)}, f32[6,4,34,1]{2,1,3,0:T(4,128)S(1)}, u32[]{:S(2)}, u32[]{:S(2)}) collective-permute-start(f32[6,4,34,1]{2,1,3,0:T(4,128)S(1)} %copy.134), channel_id=1, source_target_pairs={{0,1},{1,2},{2,3},{3,4},{4,5},{5,6},{6,7},{7,8},{8,9},{9,10},{10,1... | collective-permute-start | bytes 9800 | tf_op jit(solution)/shard_map/ppermute | solution.py:20
  116.3 3.8 %collective-permute-start.3 = (f32[6,4,34,1]{2,1,3,0:T(4,128)S(1)}, f32[6,4,34,1]{2,1,3,0:T(4,128)S(1)}, u32[]{:S(2)}, u32[]{:S(2)}) collective-permute-start(f32[6,4,34,1]{2,1,3,0:T(4,128)S(1)} %copy.135), channel_id=1, source_target_pairs={{1,0},{2,1},{3,2},{4,3},{5,4},{6,5},{7,6},{8,7},{9,8},{10,9},{11,1... | collective-permute-start | bytes 9800 | tf_op jit(solution)/shard_map/ppermute | solution.py:22
  120.2 1.1 copy.136
  121.3 1.1 copy.137
  122.4 1.7 pad_maximum_fusion.13
  124.1 5.1 %scatter.6 = f32[6,4,34,130]{3,2,1,0:T(8,128)S(1)} dynamic-update-slice(f32[6,4,34,130]{3,2,1,0:T(8,128)S(1)} %pad_maximum_fusion.13, f32[6,4,1,128]{3,2,1,0:T(1,128)S(1)} %broadcast_select_fusion.1, s32[]{:T(128)} %constant.156.clone.1, s32[]{:T(128)} %constant.156.clone.1, s32[]{:T(128)} %bitcast.5, s32[]{:T(128)} %bitcast.6) | dynamic-update-slice | bytes 24580 | tf_op jit(solution)/shard_map/scatter | solution.py:103
  129.3 3.8 %scatter.9 = f32[6,4,34,130]{3,2,1,0:T(8,128)S(1)} dynamic-update-slice(f32[6,4,34,130]{3,2,1,0:T(8,128)S(1)} %scatter.6, f32[6,4,1,128]{3,2,1,0:T(1,128)S(1)} %broadcast_select_fusion, s32[]{:T(128)} %constant.156.clone.1, s32[]{:T(128)} %constant.156.clone.1, s32[]{:T(128)} %constant.158.clone.1, s32[]{:T(128)} %constant.159.clone.1) | dynamic-update-slice | bytes 24580 | tf_op jit(solution)/shard_map/scatter | solution.py:104
  133.6 2.8 %fusion.7 = f32[32,2,5,4,128]{4,0,3,2,1:T(8,128)S(1)} fusion(f32[32,2,5,4,128]{4,0,3,2,1:T(8,128)S(1)} %fusion.29, f32[32,2,5,4,256]{4,3,2,1,0:T(4,128)} %all-to-all-done, s32[128]{0:T(128)S(1)} %get-tuple-element.79, s32[128]{0:T(128)S(1)} %broadcast_add_fusion.1, s32[128]{0:T(128)S(1)} %get-tuple-element.78, pred[128]{0:T(512)(128)(4,1)S(1)} %iota_compare_fusion.16, ...), kind=kOutput, calls=%fused_computation.22 | convolution fusion | flops 503840768 | bytes 2623360 | tf_op jit(solution)/shard_map/gsfzw,wk->gsfzk/dot_general | solution.py:136
  136.9 1.2 fusion.28
  138.1 35.8 %all-to-all-done.2 = f32[32,2,5,4,256]{4,3,2,1,0:T(4,128)} async-done(((f32[32,2,5,4,256]{4,3,2,1,0:T(4,128)}), f32[32,2,5,4,256]{4,3,2,1,0:T(4,128)}, u32[]{:S(2)}, u32[]{:S(2)}) %all-to-all-start.2) | async-done | bytes 1310752 | tf_op jit(solution)/shard_map/all_to_all | solution.py:139
  173.9 2.7 %fusion.19 = f32[16,5,4,4,256]{4,0,2,1,3:T(8,128)} fusion(f32[16,5,4,4,256]{4,0,2,1,3:T(8,128)} %fusion.2, f32[64,5,4,256]{3,2,1,0:T(4,128)} %bitcast.36, f32[16,5,4,4,256]{4,0,2,1,3:T(8,128)S(1)} %copy.142, s32[16]{0:T(128)S(1)} %multiply_add_fusion.2), kind=kOutput, calls=%fused_computation.27 | convolution fusion | flops 63079424 | bytes 2293824 | tf_op jit(solution)/shard_map/ts,sfzw->tfzw/dot_general | solution.py:145
  176.6 2.2 %multiply_add_fusion = f32[16,5,4,4,256]{4,0,2,1,3:T(8,128)S(1)} fusion(f32[16,5,4,4,256]{4,0,2,1,3:T(8,128)} %fusion.19, f32[16,5,4,4,256]{4,3,2,1,0:T(4,128)S(1)} %copy-done.1), kind=kLoop, calls=%fused_computation.21 | loop fusion | flops 655360 | bytes 3932160 | tf_op jit(solution)/shard_map/add | solution.py:153
  178.8 1.9 %copy.166 = f32[16,5,4,4,256]{4,3,2,1,0:T(4,128)} copy(f32[16,5,4,4,256]{4,0,2,1,3:T(8,128)S(1)} %multiply_add_fusion) | data formatting | bytes 2621440
  (52 shorter events, 6.7 us)
Async XLA Ops:
  4.5 27.9 %all-to-all-start.1 = ((f32[32,2,32]{2,1,0:T(2,128)}), f32[32,2,32]{2,1,0:T(2,128)S(1)}, u32[]{:S(2)}, u32[]{:S(2)}) async-start(f32[32,2,32]{2,1,0:T(2,128)} %bitcast.19), calls=%async_computation.1 | async-start | bytes 65536 | tf_op jit(solution)/shard_map/all_to_all | solution.py:135
  25.5 13.3 %copy-start = (f32[5,4,32,128]{3,2,1,0:T(8,128)S(1)}, f32[5,4,32,128]{3,2,1,0:T(8,128)}, u32[]{:S(2)}) copy-start(f32[5,4,32,128]{3,2,1,0:T(8,128)} %param.14) | copy-start | bytes 983044
  25.5 13.3 %copy-start.2 = (f32[4,32,128]{2,1,0:T(8,128)S(1)}, f32[4,32,128]{2,1,0:T(8,128)}, u32[]{:S(2)}) copy-start(f32[4,32,128]{2,1,0:T(8,128)} %param.15) | copy-start | bytes 196612
  25.5 19.2 %copy-start.3 = (f32[16,4,4,256]{3,2,1,0:T(4,128)S(1)}, f32[16,4,4,256]{3,2,1,0:T(4,128)}, u32[]{:S(2)}) copy-start(f32[16,4,4,256]{3,2,1,0:T(4,128)} %param.19) | copy-start | bytes 786436
  32.3 71.6 %all-to-all-start = ((f32[32,2,5,4,256]{4,3,2,1,0:T(4,128)}), f32[32,2,5,4,256]{4,3,2,1,0:T(4,128)}, u32[]{:S(2)}, u32[]{:S(2)}) async-start(f32[32,2,5,4,256]{4,3,2,1,0:T(4,128)} %copy.143), calls=%async_computation | async-start | bytes 2621440 | tf_op jit(solution)/shard_map/all_to_all | solution.py:134
  38.8 74.8 %collective-permute-start = (f32[6,4,1,128]{3,2,1,0:T(1,128)S(1)}, f32[6,4,1,128]{3,2,1,0:T(1,128)S(1)}, u32[]{:S(2)}, u32[]{:S(2)}) collective-permute-start(f32[6,4,1,128]{3,2,1,0:T(1,128)S(1)} %get-tuple-element.74), channel_id=1, source_target_pairs={{0,16},{16,32},{32,48},{48,64},{64,80},{80,96},{96,112},{112,128},... | collective-permute-start | bytes 36872 | tf_op jit(solution)/shard_map/ppermute | solution.py:20
  42.2 4.1 %copy-start.4 = (f32[5,4,32]{2,1,0:T(4,128)S(1)}, f32[5,4,32]{2,1,0:T(4,128)}, u32[]{:S(2)}) copy-start(f32[5,4,32]{2,1,0:T(4,128)} %param.16) | copy-start | bytes 7684
  42.2 71.4 %collective-permute-start.1 = (f32[6,4,1,128]{3,2,1,0:T(1,128)S(1)}, f32[6,4,1,128]{3,2,1,0:T(1,128)S(1)}, u32[]{:S(2)}, u32[]{:S(2)}) collective-permute-start(f32[6,4,1,128]{3,2,1,0:T(1,128)S(1)} %get-tuple-element.75), channel_id=1, source_target_pairs={{16,0},{32,16},{48,32},{64,48},{80,64},{96,80},{112,96},{128,112},... | collective-permute-start | bytes 36872 | tf_op jit(solution)/shard_map/ppermute | solution.py:22
  103.9 70.0 %all-to-all-start.2 = ((f32[32,2,5,4,256]{4,3,2,1,0:T(4,128)}), f32[32,2,5,4,256]{4,3,2,1,0:T(4,128)}, u32[]{:S(2)}, u32[]{:S(2)}) async-start(f32[32,2,5,4,256]{4,3,2,1,0:T(4,128)} %copy.163), calls=%async_computation.2 | async-start | bytes 2621440 | tf_op jit(solution)/shard_map/all_to_all | solution.py:139
  108.6 0.7 copy-start.5
  114.1 6.0 %collective-permute-start.2 = (f32[6,4,34,1]{2,1,3,0:T(4,128)S(1)}, f32[6,4,34,1]{2,1,3,0:T(4,128)S(1)}, u32[]{:S(2)}, u32[]{:S(2)}) collective-permute-start(f32[6,4,34,1]{2,1,3,0:T(4,128)S(1)} %copy.134), channel_id=1, source_target_pairs={{0,1},{1,2},{2,3},{3,4},{4,5},{5,6},{6,7},{7,8},{8,9},{9,10},{10,1... | collective-permute-start | bytes 9800 | tf_op jit(solution)/shard_map/ppermute | solution.py:20
  116.3 5.0 %collective-permute-start.3 = (f32[6,4,34,1]{2,1,3,0:T(4,128)S(1)}, f32[6,4,34,1]{2,1,3,0:T(4,128)S(1)}, u32[]{:S(2)}, u32[]{:S(2)}) collective-permute-start(f32[6,4,34,1]{2,1,3,0:T(4,128)S(1)} %copy.135), channel_id=1, source_target_pairs={{1,0},{2,1},{3,2},{4,3},{5,4},{6,5},{7,6},{8,7},{9,8},{10,9},{11,1... | collective-permute-start | bytes 9800 | tf_op jit(solution)/shard_map/ppermute | solution.py:22
  138.1 38.5 %copy-start.1 = (f32[16,5,4,4,256]{4,3,2,1,0:T(4,128)S(1)}, f32[16,5,4,4,256]{4,3,2,1,0:T(4,128)}, u32[]{:S(2)}) copy-start(f32[16,5,4,4,256]{4,3,2,1,0:T(4,128)} %param.18) | copy-start | bytes 3932164
where the time goes:
time: 181 us
  waiting for transfers between devices  70.1 us (39%)
  starting transfers between devices  38.9 us (21%)
  local copies, waits for them, and re-layouts  24.8 us (14%)
  blocking collectives  24 us (13%)
  other arithmetic  11.4 us (6%)
  matrix products  10.6 us (6%)
    all_to_all x1, waiting for transfers between devices, on_device(): lax.all_to_all(answer, 'gx', split_axis=0, concat_axis=0, tiled=True)  35.8 us
    all_to_all x1, waiting for transfers between devices, on_device(): lax.all_to_all(sending, 'gx', split_axis=0, concat_axis=0, tiled=True)  27.4 us
    all_gather x1, blocking collectives, on_device(): lax.all_gather(precursor, 'gy', axis=2, tiled=True)  24 us
    all_to_all x1, starting transfers between devices, on_device(): lax.all_to_all(columns_out, 'gx', split_axis=0, concat_axis=0, tiled=True)  16.3 us
    all_to_all x1, waiting for transfers between devices, on_device(): lax.all_to_all(columns_out, 'gx', split_axis=0, concat_axis=0, tiled=True)  6.83 us
    all_to_all x1, starting transfers between devices, on_device(): lax.all_to_all(sending, 'gx', split_axis=0, concat_axis=0, tiled=True)  6.45 us
    ppermute x2, starting transfers between devices, padded_2(): lax.ppermute(head, axis, [((i + 1) % count, i) for i in range(count)])  6.29 us
    ppermute x2, starting transfers between devices, padded_2(): lax.ppermute(tail, axis, [(i, (i + 1) % count) for i in range(count)])  5.29 us
  transfers between devices with their start and end apart: 7, of which 4 were waited for; matrix products, arithmetic and copies ran while one was open for 20% of the time, Pallas kernels for 0%

commit v1 on v0

--- a/solution.py
+++ b/solution.py
@@ -8,6 +8,13 @@
 vertical_mix = 0.1
 coarse_penalty = 0.5
 fine_penalty = 1.0
+
+
+def exchange_gather(x, mesh_axis, along):
+    size = lax.axis_size(mesh_axis)
+    tiles = jnp.stack([x for _ in range(size)])
+    tiles = lax.all_to_all(tiles, mesh_axis, split_axis=0, concat_axis=0)
+    return jnp.concatenate(tiles, axis=along)
 
 
 def padded_2(cells, sides, width):
@@ -90,10 +97,7 @@
         jnp.float32
     )
     inflow = jnp.einsum(
-        "fzp,yp->fzy",
-        lax.all_gather(precursor, "gy", axis=2, tiled=True),
-        choose,
-        precision=highest,
+        "fzp,yp->fzy", exchange_gather(precursor, "gy", 2), choose, precision=highest
     )
     stacked = jnp.concatenate([fields, viscosity[None]], axis=0)
     padded = padded_2(stacked, (("gx", 2), ("gy", 3)), 1)

time: 181 us -> 197 us (1.088)
  the two profiles are of different devices: /device:TPU:58 before, /device:TPU:40 now
where the time goes in v1:
time: 197 us; the launch traced here: 196 us
  waiting for transfers between devices  87.9 us (45%)
  starting transfers between devices  49.9 us (25%)
  local copies, waits for them, and re-layouts  28.8 us (15%)
  other arithmetic  16.7 us (8%)
  matrix products  11.9 us (6%)
    all_to_all x1, waiting for transfers between devices, on_device(): lax.all_to_all(sending, 'gx', split_axis=0, concat_axis=0, tiled=True)  49.1 us
    all_to_all x1, waiting for transfers between devices, on_device(): lax.all_to_all(answer, 'gx', split_axis=0, concat_axis=0, tiled=True)  25.2 us
    all_to_all x1, starting transfers between devices, on_device(): lax.all_to_all(columns_out, 'gx', split_axis=0, concat_axis=0, tiled=True)  16.3 us
    ppermute x2, starting transfers between devices, padded_2(): lax.ppermute(head, axis, [((i + 1) % count, i) for i in range(count)])  9.89 us
    all_to_all x1, waiting for transfers between devices, on_device(): lax.all_to_all(columns_out, 'gx', split_axis=0, concat_axis=0, tiled=True)  8.7 us
    all_to_all x1, starting transfers between devices, on_device(): lax.all_to_all(sending, 'gx', split_axis=0, concat_axis=0, tiled=True)  6.9 us
    all_to_all x1, starting transfers between devices, exchange_gather(): tiles = lax.all_to_all(tiles, mesh_axis, split_axis=0, concat_axis=0)  6.14 us
    unnamed x37, local copies, waits for them, and re-layouts  5.85 us
  transfers between devices with their start and end apart: 8, of which 4 were waited for; matrix products, arithmetic and copies ran while one was open for 23% of the time, Pallas kernels for 0%

profile of v1, /device:TPU:40, one launch (start us, length us, event | category | flops | bytes accessed | tf_op | source)
XLA Modules:
  0.0 196.2 jit_solution(12936528930870753441)
XLA Ops:
  2.9 1.6 fusion.89
  4.5 16.3 %all-to-all-start.2 = ((f32[32,2,32]{2,1,0:T(2,128)}), f32[32,2,32]{2,1,0:T(2,128)S(1)}, u32[]{:S(2)}, u32[]{:S(2)}) async-start(f32[32,2,32]{2,1,0:T(2,128)} %bitcast.20), calls=%async_computation.2 | async-start | bytes 65536 | tf_op jit(solution)/shard_map/all_to_all | solution.py:139
  20.7 2.1 %copy.142 = f32[16,5,4,4,256]{4,0,2,1,3:T(8,128)S(1)} copy(f32[16,5,4,4,256]{4,3,2,1,0:T(4,128)} %param.18) | data formatting | bytes 2621440 | tf_op args[4]
  23.6 8.7 %all-to-all-done.2 = f32[32,2,32]{2,1,0:T(2,128)S(1)} async-done(((f32[32,2,32]{2,1,0:T(2,128)}), f32[32,2,32]{2,1,0:T(2,128)S(1)}, u32[]{:S(2)}, u32[]{:S(2)}) %all-to-all-start.2) | async-done | bytes 8224 | tf_op jit(solution)/shard_map/all_to_all | solution.py:139
  32.3 6.1 %all-to-all-start = ((f32[16,1,640]{2,1,0:T(1,128)}), f32[16,1,640]{2,1,0:T(1,128)S(1)}, u32[]{:S(2)}, u32[]{:S(2)}) async-start(f32[16,1,640]{2,1,0:T(1,128)} %reshape.265), calls=%async_computation | async-start | bytes 81920 | tf_op jit(solution)/shard_map/all_to_all | solution.py:16
  39.3 1.9 copy.143
  41.2 4.9 %all-to-all-done = f32[16,1,640]{2,1,0:T(1,128)S(1)} async-done(((f32[16,1,640]{2,1,0:T(1,128)}), f32[16,1,640]{2,1,0:T(1,128)S(1)}, u32[]{:S(2)}, u32[]{:S(2)}) %all-to-all-start) | async-done | bytes 40992 | tf_op jit(solution)/shard_map/all_to_all | solution.py:16
  46.1 6.9 %all-to-all-start.1 = ((f32[32,2,5,4,256]{4,3,2,1,0:T(4,128)}), f32[32,2,5,4,256]{4,3,2,1,0:T(4,128)}, u32[]{:S(2)}, u32[]{:S(2)}) async-start(f32[32,2,5,4,256]{4,3,2,1,0:T(4,128)} %copy.143), calls=%async_computation.1 | async-start | bytes 2621440 | tf_op jit(solution)/shard_map/all_to_all | solution.py:138
  53.6 3.4 %collective-permute-start = (f32[6,4,1,128]{3,2,1,0:T(1,128)S(1)}, f32[6,4,1,128]{3,2,1,0:T(1,128)S(1)}, u32[]{:S(2)}, u32[]{:S(2)}) collective-permute-start(f32[6,4,1,128]{3,2,1,0:T(1,128)S(1)} %get-tuple-element.74), channel_id=1, source_target_pairs={{0,16},{16,32},{32,48},{48,64},{64,80},{80,96},{96,112},{112,128},... | collective-permute-start | bytes 36872 | tf_op jit(solution)/shard_map/ppermute | solution.py:27
  57.0 2.5 %collective-permute-start.1 = (f32[6,4,1,128]{3,2,1,0:T(1,128)}, f32[6,4,1,128]{3,2,1,0:T(1,128)S(1)}, u32[]{:S(2)}, u32[]{:S(2)}) collective-permute-start(f32[6,4,1,128]{3,2,1,0:T(1,128)} %get-tuple-element.75), channel_id=1, source_target_pairs={{16,0},{32,16},{48,32},{64,48},{80,64},{96,80},{112,96},{128,112},... | collective-permute-start | bytes 36872 | tf_op jit(solution)/shard_map/ppermute | solution.py:29
  59.7 1.1 slice_bitcast_fusion.1
  60.7 0.9 copy.156
  65.6 1.8 fusion.49
  67.5 1.9 copy.163
  69.4 49.1 %all-to-all-done.1 = f32[32,2,5,4,256]{4,3,2,1,0:T(4,128)} async-done(((f32[32,2,5,4,256]{4,3,2,1,0:T(4,128)}), f32[32,2,5,4,256]{4,3,2,1,0:T(4,128)}, u32[]{:S(2)}, u32[]{:S(2)}) %all-to-all-start.1) | async-done | bytes 1310752 | tf_op jit(solution)/shard_map/all_to_all | solution.py:138
  118.5 5.5 %all-to-all-start.3 = ((f32[32,2,5,4,256]{4,3,2,1,0:T(4,128)}), f32[32,2,5,4,256]{4,3,2,1,0:T(4,128)}, u32[]{:S(2)}, u32[]{:S(2)}) async-start(f32[32,2,5,4,256]{4,3,2,1,0:T(4,128)} %copy.163), calls=%async_computation.3 | async-start | bytes 2621440 | tf_op jit(solution)/shard_map/all_to_all | solution.py:143
  127.2 3.0 %fusion.2 = f32[16,5,4,4,256]{4,0,2,1,3:T(8,128)} fusion(f32[16,5,1,4,256]{4,0,2,1,3:T(8,128)S(1)} %get-tuple-element.59, f32[16,5,3,4,256]{4,0,2,1,3:T(8,128)S(1)} %get-tuple-element.61, f32[16,5,3,4,256]{4,0,2,1,3:T(8,128)S(1)} %get-tuple-element.60, f32[16,5,1,4,256]{4,0,2,1,3:T(8,128)S(1)} %get-tuple-element.58, f32[16,5,4,4,256]{4,0,2,1,3:T(8,128)S(1)} %copy.142, ...), kind=kLoop, calls=%fused_computation.16 | loop fusion | flops 12124160 | bytes 7882752 | tf_op jit(solution)/shard_map/add | solution.py:61
  131.2 1.9 collective-permute-start.2
  133.4 7.4 %collective-permute-start.3 = (f32[6,4,34,1]{2,1,3,0:T(4,128)S(1)}, f32[6,4,34,1]{2,1,3,0:T(4,128)S(1)}, u32[]{:S(2)}, u32[]{:S(2)}) collective-permute-start(f32[6,4,34,1]{2,1,3,0:T(4,128)S(1)} %copy.135), channel_id=1, source_target_pairs={{1,0},{2,1},{3,2},{4,3},{5,4},{6,5},{7,6},{8,7},{9,8},{10,9},{11,1... | collective-permute-start | bytes 9800 | tf_op jit(solution)/shard_map/ppermute | solution.py:29
  141.4 1.1 copy.136
  142.5 1.1 copy.137
  143.6 1.7 pad_maximum_fusion.13
  147.4 1.0 reshape.264
  148.4 1.0 fusion.43
  150.2 5.0 %scatter.6 = f32[6,4,34,130]{3,2,1,0:T(8,128)S(1)} dynamic-update-slice(f32[6,4,34,130]{3,2,1,0:T(8,128)S(1)} %pad_maximum_fusion.13, f32[6,4,1,128]{3,2,1,0:T(1,128)S(1)} %broadcast_select_fusion.1, s32[]{:T(128)} %constant.156.clone.1, s32[]{:T(128)} %constant.156.clone.1, s32[]{:T(128)} %bitcast.6, s32[]{:T(128)} %bitcast.7) | dynamic-update-slice | bytes 24580 | tf_op jit(solution)/shard_map/scatter | solution.py:107
  155.3 3.8 %scatter.9 = f32[6,4,34,130]{3,2,1,0:T(8,128)S(1)} dynamic-update-slice(f32[6,4,34,130]{3,2,1,0:T(8,128)S(1)} %scatter.6, f32[6,4,1,128]{3,2,1,0:T(1,128)S(1)} %broadcast_select_fusion, s32[]{:T(128)} %constant.156.clone.1, s32[]{:T(128)} %constant.156.clone.1, s32[]{:T(128)} %constant.158.clone.1, s32[]{:T(128)} %constant.159.clone.1) | dynamic-update-slice | bytes 24580 | tf_op jit(solution)/shard_map/scatter | solution.py:108
  159.7 2.8 %fusion.7 = f32[32,2,5,4,128]{4,0,3,2,1:T(8,128)S(1)} fusion(f32[32,2,5,4,128]{4,0,3,2,1:T(8,128)S(1)} %fusion.29, f32[32,2,5,4,256]{4,3,2,1,0:T(4,128)} %all-to-all-done.1, s32[128]{0:T(128)S(1)} %copy-done.12, s32[128]{0:T(128)S(1)} %copy-done.13, s32[128]{0:T(128)S(1)} %copy-done.11, pred[128]{0:T(512)(128)(4,1)S(1)} %copy-done.15, ...), kind=kOutput, calls=%fused_computation.22 | convolution fusion | flops 503840768 | bytes 2623360 | tf_op jit(solution)/shard_map/gsfzw,wk->gsfzk/dot_general | solution.py:140
  163.0 1.2 fusion.28
  164.2 25.2 %all-to-all-done.3 = f32[32,2,5,4,256]{4,3,2,1,0:T(4,128)} async-done(((f32[32,2,5,4,256]{4,3,2,1,0:T(4,128)}), f32[32,2,5,4,256]{4,3,2,1,0:T(4,128)}, u32[]{:S(2)}, u32[]{:S(2)}) %all-to-all-start.3) | async-done | bytes 1310752 | tf_op jit(solution)/shard_map/all_to_all | solution.py:143
  189.4 2.7 %fusion.19 = f32[16,5,4,4,256]{4,0,2,1,3:T(8,128)} fusion(f32[16,5,4,4,256]{4,0,2,1,3:T(8,128)} %fusion.2, f32[64,5,4,256]{3,2,1,0:T(4,128)} %bitcast.37, f32[16,5,4,4,256]{4,0,2,1,3:T(8,128)S(1)} %copy.142, s32[16]{0:T(128)S(1)} %copy-done.10), kind=kOutput, calls=%fused_computation.27 | convolution fusion | flops 63079424 | bytes 2293824 | tf_op jit(solution)/shard_map/ts,sfzw->tfzw/dot_general | solution.py:149
  192.1 2.2 %multiply_add_fusion = f32[16,5,4,4,256]{4,0,2,1,3:T(8,128)S(1)} fusion(f32[16,5,4,4,256]{4,0,2,1,3:T(8,128)} %fusion.19, f32[16,5,4,4,256]{4,3,2,1,0:T(4,128)S(1)} %copy-done.1), kind=kLoop, calls=%fused_computation.21 | loop fusion | flops 655360 | bytes 3932160 | tf_op jit(solution)/shard_map/add | solution.py:157
  194.3 1.9 copy.166
  (78 shorter events, 17.6 us)
Async XLA Ops:
  2.9 35.6 %copy-start.9 = (s32[16]{0:T(128)}, s32[16]{0:T(128)S(1)}, u32[]{:S(2)}) copy-start(s32[16]{0:T(128)S(1)} %multiply_add_fusion.2) | copy-start | bytes 196
  4.5 27.9 %all-to-all-start.2 = ((f32[32,2,32]{2,1,0:T(2,128)}), f32[32,2,32]{2,1,0:T(2,128)S(1)}, u32[]{:S(2)}, u32[]{:S(2)}) async-start(f32[32,2,32]{2,1,0:T(2,128)} %bitcast.20), calls=%async_computation.2 | async-start | bytes 65536 | tf_op jit(solution)/shard_map/all_to_all | solution.py:139
  20.7 2.1 %copy-start.8 = (f32[5,4,32]{2,1,0:T(4,128)S(1)}, f32[5,4,32]{2,1,0:T(4,128)}, u32[]{:S(2)}) copy-start(f32[5,4,32]{2,1,0:T(4,128)} %param.16) | copy-start | bytes 7684
  32.3 13.8 %all-to-all-start = ((f32[16,1,640]{2,1,0:T(1,128)}), f32[16,1,640]{2,1,0:T(1,128)S(1)}, u32[]{:S(2)}, u32[]{:S(2)}) async-start(f32[16,1,640]{2,1,0:T(1,128)} %reshape.265), calls=%async_computation | async-start | bytes 81920 | tf_op jit(solution)/shard_map/all_to_all | solution.py:16
  41.2 11.8 %copy-start = (f32[5,4,32,128]{3,2,1,0:T(8,128)S(1)}, f32[5,4,32,128]{3,2,1,0:T(8,128)}, u32[]{:S(2)}) copy-start(f32[5,4,32,128]{3,2,1,0:T(8,128)} %param.14) | copy-start | bytes 983044
  41.2 11.8 %copy-start.4 = (f32[4,32,128]{2,1,0:T(8,128)S(1)}, f32[4,32,128]{2,1,0:T(8,128)}, u32[]{:S(2)}) copy-start(f32[4,32,128]{2,1,0:T(8,128)} %param.15) | copy-start | bytes 196612
  41.2 18.3 %copy-start.5 = (f32[16,4,4,256]{3,2,1,0:T(4,128)S(1)}, f32[16,4,4,256]{3,2,1,0:T(4,128)}, u32[]{:S(2)}) copy-start(f32[16,4,4,256]{3,2,1,0:T(4,128)} %param.19) | copy-start | bytes 786436
  46.1 72.4 %all-to-all-start.1 = ((f32[32,2,5,4,256]{4,3,2,1,0:T(4,128)}), f32[32,2,5,4,256]{4,3,2,1,0:T(4,128)}, u32[]{:S(2)}, u32[]{:S(2)}) async-start(f32[32,2,5,4,256]{4,3,2,1,0:T(4,128)} %copy.143), calls=%async_computation.1 | async-start | bytes 2621440 | tf_op jit(solution)/shard_map/all_to_all | solution.py:138
  53.6 8.8 %copy-start.7 = (f32[6,4,1,128]{3,2,1,0:T(1,128)}, f32[6,4,1,128]{3,2,1,0:T(1,128)S(1)}, u32[]{:S(2)}) copy-start(f32[6,4,1,128]{3,2,1,0:T(1,128)S(1)} %get-tuple-element.74) | copy-start | bytes 36868
  53.6 77.0 %collective-permute-start = (f32[6,4,1,128]{3,2,1,0:T(1,128)S(1)}, f32[6,4,1,128]{3,2,1,0:T(1,128)S(1)}, u32[]{:S(2)}, u32[]{:S(2)}) collective-permute-start(f32[6,4,1,128]{3,2,1,0:T(1,128)S(1)} %get-tuple-element.74), channel_id=1, source_target_pairs={{0,16},{16,32},{32,48},{48,64},{64,80},{80,96},{96,112},{112,128},... | collective-permute-start | bytes 36872 | tf_op jit(solution)/shard_map/ppermute | solution.py:27
  57.0 73.7 %collective-permute-start.1 = (f32[6,4,1,128]{3,2,1,0:T(1,128)}, f32[6,4,1,128]{3,2,1,0:T(1,128)S(1)}, u32[]{:S(2)}, u32[]{:S(2)}) collective-permute-start(f32[6,4,1,128]{3,2,1,0:T(1,128)} %get-tuple-element.75), channel_id=1, source_target_pairs={{16,0},{32,16},{48,32},{64,48},{80,64},{96,80},{112,96},{128,112},... | collective-permute-start | bytes 36872 | tf_op jit(solution)/shard_map/ppermute | solution.py:29
  118.5 70.9 %all-to-all-start.3 = ((f32[32,2,5,4,256]{4,3,2,1,0:T(4,128)}), f32[32,2,5,4,256]{4,3,2,1,0:T(4,128)}, u32[]{:S(2)}, u32[]{:S(2)}) async-start(f32[32,2,5,4,256]{4,3,2,1,0:T(4,128)} %copy.163), calls=%async_computation.3 | async-start | bytes 2621440 | tf_op jit(solution)/shard_map/all_to_all | solution.py:143
  126.1 1.0 copy-start.2
  126.1 1.0 copy-start.3
  130.7 12.9 %copy-start.6 = (f32[6,4,1,128]{3,2,1,0:T(1,128)}, f32[6,4,1,128]{3,2,1,0:T(1,128)S(1)}, u32[]{:S(2)}) copy-start(f32[6,4,1,128]{3,2,1,0:T(1,128)S(1)} %collective-permute-done) | copy-start | bytes 36868
  131.2 10.2 %collective-permute-start.2 = (f32[6,4,34,1]{2,1,3,0:T(4,128)S(1)}, f32[6,4,34,1]{2,1,3,0:T(4,128)S(1)}, u32[]{:S(2)}, u32[]{:S(2)}) collective-permute-start(f32[6,4,34,1]{2,1,3,0:T(4,128)S(1)} %copy.134), channel_id=1, source_target_pairs={{0,1},{1,2},{2,3},{3,4},{4,5},{5,6},{6,7},{7,8},{8,9},{9,10},{10,1... | collective-permute-start | bytes 9800 | tf_op jit(solution)/shard_map/ppermute | solution.py:27
  133.4 9.1 %collective-permute-start.3 = (f32[6,4,34,1]{2,1,3,0:T(4,128)S(1)}, f32[6,4,34,1]{2,1,3,0:T(4,128)S(1)}, u32[]{:S(2)}, u32[]{:S(2)}) collective-permute-start(f32[6,4,34,1]{2,1,3,0:T(4,128)S(1)} %copy.135), channel_id=1, source_target_pairs={{1,0},{2,1},{3,2},{4,3},{5,4},{6,5},{7,6},{8,7},{9,8},{10,9},{11,1... | collective-permute-start | bytes 9800 | tf_op jit(solution)/shard_map/ppermute | solution.py:29
  147.4 12.2 %copy-start.11 = (s32[128]{0:T(128)S(1)}, s32[128]{0:T(128)}, u32[]{:S(2)}) copy-start(s32[128]{0:T(128)} %get-tuple-element.78) | copy-start | bytes 1540
  147.4 12.2 %copy-start.12 = (s32[128]{0:T(128)S(1)}, s32[128]{0:T(128)}, u32[]{:S(2)}) copy-start(s32[128]{0:T(128)} %get-tuple-element.79) | copy-start | bytes 1540
  147.4 12.3 %copy-start.13 = (s32[128]{0:T(128)S(1)}, s32[128]{0:T(128)}, u32[]{:S(2)}) copy-start(s32[128]{0:T(128)} %broadcast_add_fusion.1) | copy-start | bytes 1540
  147.4 12.3 %copy-start.14 = (pred[256]{0:T(512)(128)(4,1)S(1)}, pred[256]{0:T(512)(128)(4,1)}, u32[]{:S(2)}) copy-start(pred[256]{0:T(512)(128)(4,1)} %iota_compare_fusion.15) | copy-start | bytes 772
  147.4 12.3 %copy-start.15 = (pred[128]{0:T(512)(128)(4,1)S(1)}, pred[128]{0:T(512)(128)(4,1)}, u32[]{:S(2)}) copy-start(pred[128]{0:T(512)(128)(4,1)} %iota_compare_fusion.16) | copy-start | bytes 388
  162.9 26.4 %copy-start.10 = (s32[16]{0:T(128)S(1)}, s32[16]{0:T(128)}, u32[]{:S(2)}) copy-start(s32[16]{0:T(128)} %copy-done.9) | copy-start | bytes 196
  164.2 27.9 %copy-start.1 = (f32[16,5,4,4,256]{4,3,2,1,0:T(4,128)S(1)}, f32[16,5,4,4,256]{4,3,2,1,0:T(4,128)}, u32[]{:S(2)}) copy-start(f32[16,5,4,4,256]{4,3,2,1,0:T(4,128)} %param.18) | copy-start | bytes 3932164
